TPU v7x, 512 devices: a whole 4x8x8 slice. The times are simulated.
512 devices in a mesh: fsdp: 16 (over y, x_lo), ed: 32 (over x_hi, z, core).
Axes of the slice: x: 4 (x_hi: 2, x_lo: 2; x = x_hi * 2 + x_lo), y: 8, z: 8, core: 2. Of those that a mesh axis runs over, the one named last changes fastest.
Arguments:
- tokens: bfloat16 [9216, 6144], P('ed', 'fsdp'), may hold values from -6 to 6
- expert_ids: int32 [9216, 2], P('ed'), may hold values from 0 to 7, all different within a row; in each aligned block of 288 rows (0 to 287, 288 to 575, ...) at most 81 rows name the same one
- route_weights: float32 [9216, 2], P('ed'), may hold values from 0.1 to 1
- w_gate: bfloat16 [1, 6144, 8192], P(None, 'fsdp', 'ed'), may hold values from -0.078125 to 0.078125
- w_up: bfloat16 [1, 6144, 8192], P(None, 'fsdp', 'ed'), may hold values from -0.078125 to 0.078125
- w_down: bfloat16 [1, 8192, 6144], P(None, 'ed', 'fsdp'), may hold values from -0.0625 to 0.0625
Outputs:
- mixed: bfloat16 [9216, 6144], P('ed', 'fsdp')
Inputs may be any that keep to these rules, and one draw needn't show every extreme that they name: `expert_ids`: each row names two different experts. In each block of 288 rows that one index of ed holds, no expert is named by more than 81 rows, a bound that some block reaches.
All inputs are finite; a program needn't handle non-finite values.
Results may differ from a plain program's by a relative error of at most 0.025.
Values may be sent and summed in bfloat16 or wider, within the bound.
A program may use at most 64 MiB of HBM per device.

v0:
```python
import jax
import jax.numpy as jnp
from jax import lax
from jax.sharding import PartitionSpec as P

CAP = 81


def slot_match(routes, window, capacity):
    window_ids = jnp.arange(window, dtype=jnp.int32)
    routed = jnp.any(routes[:, :, None, :] == window_ids[None, None, :, None], axis=3)
    position = jnp.cumsum(routed.astype(jnp.int32), axis=1) - 1
    slot_ids = jnp.arange(capacity, dtype=jnp.int32)
    hits = routed[:, :, :, None] & (position[:, :, :, None] == slot_ids[None, None, None, :])
    return hits.astype(jnp.int32)


def take_block(block_rows, row_list):
    return jnp.take(block_rows, row_list, axis=0)


def pick_rows(blocks, routes, window, capacity):
    match = slot_match(routes, window, capacity)
    row_numbers = jnp.arange(blocks.shape[1], dtype=jnp.int32)
    source_row = jnp.sum(match * row_numbers[None, :, None, None], axis=1).reshape(
        blocks.shape[0], window * capacity
    )
    filled = jnp.sum(match, axis=1).reshape(blocks.shape[0], window * capacity)
    picked = jax.vmap(take_block)(blocks, source_row)
    picked = jnp.where(filled[:, :, None] > 0, picked, jnp.zeros_like(picked))
    return picked.reshape(blocks.shape[0], window, capacity, blocks.shape[2])


def combine_matrix(routes, weights, window, capacity):
    match = slot_match(routes[None], window, capacity)[0]
    window_ids = jnp.arange(window, dtype=jnp.int32)
    per_expert = jnp.sum(
        jnp.where(
            routes[:, None, :] == window_ids[None, :, None],
            weights[:, None, :],
            jnp.zeros_like(weights[:, None, :]),
        ),
        axis=2,
    )
    return (per_expert[:, :, None] * match.astype(weights.dtype)).reshape(
        routes.shape[0], window * capacity
    )


def local(tokens, expert_ids, route_weights, w_gate, w_up, w_down):
    window = w_gate.shape[0]
    features_dev = tokens.shape[1]
    own_slots = pick_rows(tokens[None], expert_ids[None], window, CAP)[0]
    selected = lax.all_gather(own_slots, "ed", axis=1, tiled=True)
    rows_full = lax.all_to_all(selected, "fsdp", split_axis=1, concat_axis=2, tiled=True)
    gate_part = jnp.einsum(
        "hnm,hmq->hnq",
        rows_full,
        lax.all_gather(w_gate, "fsdp", axis=1, tiled=True),
        preferred_element_type=jnp.float32,
    )
    up_part = jnp.einsum(
        "hnm,hmq->hnq",
        rows_full,
        lax.all_gather(w_up, "fsdp", axis=1, tiled=True),
        preferred_element_type=jnp.float32,
    )
    activation = (jax.nn.silu(gate_part) * up_part).astype(jnp.bfloat16)
    act_one = activation[0]

    def columns_out(shard_piece, first_col, act_one=act_one):
        return jnp.dot(act_one, shard_piece, preferred_element_type=jnp.float32)

    whole_rows = columns_out(lax.all_gather(w_down[0], "fsdp", axis=1, tiled=True), jnp.int32(0))
    outputs_list = [whole_rows.astype(jnp.bfloat16)]
    stacked = jnp.stack(outputs_list)
    exchanged = lax.all_to_all(stacked, "fsdp", split_axis=2, concat_axis=1, tiled=True)
    partial_out = exchanged.astype(jnp.float32)
    slot_out = lax.psum_scatter(
        partial_out.astype(jnp.bfloat16), "ed", scatter_dimension=1, tiled=True
    ).astype(jnp.float32)
    weights_matrix = combine_matrix(expert_ids, route_weights, window, CAP)
    mixed = jnp.dot(
        weights_matrix,
        slot_out.reshape(window * CAP, features_dev),
        precision=lax.Precision.HIGHEST,
        preferred_element_type=jnp.float32,
    )
    return mixed.astype(jnp.bfloat16)


def solution(mesh):
    return jax.shard_map(
        local,
        mesh=mesh,
        in_specs=(
            P("ed", "fsdp"),
            P("ed", None),
            P("ed", None),
            P(None, "fsdp", "ed"),
            P(None, "fsdp", "ed"),
            P(None, "ed", "fsdp"),
        ),
        out_specs=P("ed", "fsdp"),
        check_vma=False,
    )
```

profile of v0, /device:TPU:1, one launch (start us, length us, event | category | flops | bytes accessed | tf_op | source)
XLA Modules:
  0.0 640.9 jit_solution(6663339600788899471)
XLA Ops:
  8.1 3.0 convert_reduce_fusion
  15.4 96.3 %all-gather.6.cloned.1.call-done = bf16[1,2592,384]{2,0,1:T(2,128)(2,1)} async-done(((bf16[1,81,384]{2,0,1:T(2,128)(2,1)}), bf16[1,2592,384]{2,0,1:T(2,128)(2,1)}) %all-gather.6.cloned.1.call-update) | async-done | bytes 1990672 | tf_op jit(solution)/shard_map/all_gather | solution.py:54
  112.2 15.8 %reduce.14 = bf16[2592,384]{1,0:T(8,128)(2,1)S(1)} reduce(bf16[2592,1,384]{2,1,0:T(2,128)(2,1)} %bitcast.80, bf16[]{:T(256)} %broadcast.283), dimensions={1}, to_apply=%bitcast.61.reduce_sub_computation | reduce | bytes 3981314
  128.0 1.6 reshape.463
  129.6 71.7 %all_to_all.33 = bf16[16,2,31104]{2,1,0:T(2,128)(2,1)S(1)} all-to-all(bf16[16,2,31104]{2,1,0:T(2,128)(2,1)} %reshape.463), channel_id=1, replica_groups=mesh['fsdp'=16,'ed'=32] {'fsdp'}, dimensions={0} | all-to-all | bytes 3981312 | tf_op jit(solution)/shard_map/all_to_all | solution.py:55
  201.2 8.9 %reshape.464 = bf16[2592,1,384]{2,1,0:T(2,128)(2,1)} reshape(bf16[16,2,31104]{2,1,0:T(2,128)(2,1)S(1)} %all_to_all.33) | data formatting | bytes 3981312
  210.2 17.6 %bitcast_reduce_fusion = bf16[2592,384]{1,0:T(8,128)(2,1)} fusion(bf16[2592,1,384]{2,1,0:T(2,128)(2,1)} %reshape.464), kind=kLoop, calls=%fused_computation.46 | loop fusion | bytes 3981312 | tf_op jit(solution)/shard_map/all_to_all | solution.py:55
  227.8 1.8 all_to_all.25
  230.6 2.7 fusion.5
  233.3 66.1 %all-gather.10.cloned.1.call-done = bf16[1,6144,256]{2,1,0:T(8,128)(2,1)} async-done(((bf16[1,384,256]{2,1,0:T(8,128)(2,1)}), bf16[1,6144,256]{2,1,0:T(8,128)(2,1)}) %all-gather.10.cloned.1.call-update) | async-done | bytes 3145744 | tf_op jit(solution)/shard_map/all_gather | solution.py:65
  299.3 85.3 %all-gather.12.cloned.1.call-done = bf16[1,256,6144]{2,1,0:T(8,128)(2,1)} async-done(((bf16[1,256,384]{2,1,0:T(8,128)(2,1)}), bf16[1,256,6144]{2,1,0:T(8,128)(2,1)}) %all-gather.12.cloned.1.call-update) | async-done | bytes 3145744 | tf_op jit(solution)/shard_map/all_gather | solution.py:74
  384.6 6.5 %fusion.1 = bf16[1,162,6144]{2,1,0:T(8,128)(2,1)} fusion(bf16[1,256,6144]{2,1,0:T(8,128)(2,1)} %all-gather.12.cloned.1.call-done, bf16[162,6144]{1,0:T(8,128)(2,1)S(1)} %bitcast.74, bf16[1,6144,256]{2,1,0:T(8,128)(2,1)} %all-gather.10.cloned.1.call-done, f32[162,256]{1,0:T(8,128)S(1)} %fusion.5), kind=kOutput, calls=%fused_computation.2 | convolution fusion | flops 1020460032 | bytes 10438656 | tf_op jit(solution)/shard_map/dot_general | solution.py:72
  391.1 13.7 %copy.20 = bf16[1,162,6144]{1,0,2:T(2,128)(2,1)} copy(bf16[1,162,6144]{2,1,0:T(8,128)(2,1)} %fusion.1) | data formatting | bytes 3981312 | tf_op jit(solution)/shard_map/stack | solution.py:76
  404.8 34.6 %reduce.15 = bf16[6144,162]{1,0:T(8,128)(2,1)S(1)} reduce(bf16[6144,1,162]{2,1,0:T(2,128)(2,1)} %bitcast.71, bf16[]{:T(256)} %broadcast.283), dimensions={1}, to_apply=%bitcast.63.reduce_sub_computation | reduce | bytes 3981314
  439.4 6.9 %reshape.465 = bf16[16,2,31104]{2,1,0:T(2,128)(2,1)} reshape(bf16[6144,162]{1,0:T(8,128)(2,1)S(1)} %reduce.15) | data formatting | bytes 3981312
  446.4 4.2 all-to-all-start.1
  450.7 42.9 %all-to-all-done.1 = bf16[16,2,31104]{2,1,0:T(2,128)(2,1)S(1)} async-done(((bf16[16,2,31104]{2,1,0:T(2,128)(2,1)}), bf16[16,2,31104]{2,1,0:T(2,128)(2,1)S(1)}, u32[]{:S(2)}, u32[]{:S(2)}) %all-to-all-start.1) | async-done | bytes 1990688 | tf_op jit(solution)/shard_map/all_to_all | solution.py:77
  493.5 12.1 %reshape.466 = bf16[6144,1,162]{2,1,0:T(2,128)(2,1)} reshape(bf16[16,2,31104]{2,1,0:T(2,128)(2,1)S(1)} %all-to-all-done.1) | data formatting | bytes 3981312
  505.6 13.8 %copy.21 = bf16[1,162,6144]{2,1,0:T(8,128)(2,1)S(1)} copy(bf16[1,162,6144]{1,0,2:T(2,128)(2,1)} %bitcast.72) | data formatting | bytes 3981312 | tf_op jit(solution)/shard_map/all_to_all | solution.py:77
  522.0 81.8 %fusion = bf16[96,384]{1,0:T(8,128)(2,1)S(1)} fusion(bf16[1,2592,384]{2,1,0:T(8,128)(2,1)} %all_to_all.30), kind=kCustom, calls=%all-reduce-scatter | all-reduce-scatter fusion | flops 1179649 | bytes 2066432
  603.9 3.5 collective-permute-start
  611.4 16.7 %collective-permute-start.4 = (bf16[81,384]{1,0:T(8,128)(2,1)S(1)}, bf16[81,384]{1,0:T(8,128)(2,1)S(1)}, u32[]{:S(2)}, u32[]{:S(2)}) collective-permute-start(bf16[81,384]{1,0:T(8,128)(2,1)S(1)} %slice.16), channel_id=1, source_target_pairs={{0,5},{1,6},{2,7},{3,8},{4,9},{5,10},{6,11},{7,12},{8,13},{9,14},{... | collective-permute-start | bytes 186632
  628.1 1.7 convert_multiply_fusion
  631.8 1.6 concatenate.3
  (55 shorter events, 16.2 us)
Async XLA Ops:
  6.5 4.6 copy-start
  6.5 105.1 %all-gather.6.cloned.1.call-start = ((), (), s32[]{:S(2)}) async-start(), calls=%async_computation.2 | async-start | bytes 4105728 | tf_op jit(solution)/shard_map/all_gather | solution.py:54
  13.3 217.3 %all-gather.8.cloned.1.call-start = ((), (), s32[]{:S(2)}) async-start(), calls=%async_computation.3 | async-start | bytes 3342336 | tf_op jit(solution)/shard_map/all_gather | solution.py:59
  14.1 285.3 %all-gather.10.cloned.1.call-start = ((), (), s32[]{:S(2)}) async-start(), calls=%async_computation.4 | async-start | bytes 3342336 | tf_op jit(solution)/shard_map/all_gather | solution.py:65
  14.8 369.8 %all-gather.12.cloned.1.call-start = ((), (), s32[]{:S(2)}) async-start(), calls=%async_computation.5 | async-start | bytes 3342336 | tf_op jit(solution)/shard_map/all_gather | solution.py:74
  446.4 4.2 copy-start.2
  446.4 4.3 copy-start.3
  446.4 47.1 %all-to-all-start.1 = ((bf16[16,2,31104]{2,1,0:T(2,128)(2,1)}), bf16[16,2,31104]{2,1,0:T(2,128)(2,1)S(1)}, u32[]{:S(2)}, u32[]{:S(2)}) async-start(bf16[16,2,31104]{2,1,0:T(2,128)(2,1)} %reshape.465), calls=%async_computation.1 | async-start | bytes 3981312 | tf_op jit(solution)/shard_map/all_to_all | solution.py:77
  520.5 113.9 %copy-start.1 = (bf16[288,384]{1,0:T(8,128)(2,1)S(1)}, bf16[288,384]{1,0:T(8,128)(2,1)}, u32[]{:S(2)}) copy-start(bf16[288,384]{1,0:T(8,128)(2,1)} %param.6) | copy-start | bytes 663556
  603.9 27.8 %collective-permute-start = (bf16[96,384]{1,0:T(8,128)(2,1)S(1)}, bf16[96,384]{1,0:T(8,128)(2,1)S(1)}, u32[]{:S(2)}, u32[]{:S(2)}) collective-permute-start(bf16[96,384]{1,0:T(8,128)(2,1)S(1)} %fusion), channel_id=1, source_target_pairs={{0,1},{1,2},{2,3},{3,4},{4,5},{5,6},{6,7},{7,8},{8,9},{9,10},{10,1... | collective-permute-start | bytes 221192
  607.5 24.3 %collective-permute-start.1 = (bf16[96,384]{1,0:T(8,128)(2,1)S(1)}, bf16[96,384]{1,0:T(8,128)(2,1)S(1)}, u32[]{:S(2)}, u32[]{:S(2)}) collective-permute-start(bf16[96,384]{1,0:T(8,128)(2,1)S(1)} %fusion), channel_id=1, source_target_pairs={{0,2},{1,3},{2,4},{3,5},{4,6},{5,7},{6,8},{7,9},{8,10},{9,11},{10,... | collective-permute-start | bytes 221192
  608.8 23.0 %collective-permute-start.2 = (bf16[96,384]{1,0:T(8,128)(2,1)S(1)}, bf16[96,384]{1,0:T(8,128)(2,1)S(1)}, u32[]{:S(2)}, u32[]{:S(2)}) collective-permute-start(bf16[96,384]{1,0:T(8,128)(2,1)S(1)} %fusion), channel_id=1, source_target_pairs={{0,3},{1,4},{2,5},{3,6},{4,7},{5,8},{6,9},{7,10},{8,11},{9,12},{10... | collective-permute-start | bytes 221192
  610.1 21.7 %collective-permute-start.3 = (bf16[96,384]{1,0:T(8,128)(2,1)S(1)}, bf16[96,384]{1,0:T(8,128)(2,1)S(1)}, u32[]{:S(2)}, u32[]{:S(2)}) collective-permute-start(bf16[96,384]{1,0:T(8,128)(2,1)S(1)} %fusion), channel_id=1, source_target_pairs={{0,4},{1,5},{2,6},{3,7},{4,8},{5,9},{6,10},{7,11},{8,12},{9,13},{1... | collective-permute-start | bytes 221192
  611.4 20.3 %collective-permute-start.4 = (bf16[81,384]{1,0:T(8,128)(2,1)S(1)}, bf16[81,384]{1,0:T(8,128)(2,1)S(1)}, u32[]{:S(2)}, u32[]{:S(2)}) collective-permute-start(bf16[81,384]{1,0:T(8,128)(2,1)S(1)} %slice.16), channel_id=1, source_target_pairs={{0,5},{1,6},{2,7},{3,8},{4,9},{5,10},{6,11},{7,12},{8,13},{9,14},{... | collective-permute-start | bytes 186632
Sparse Core Ops, SparseCore 0:
  13.4 98.1 all-gather.5
  113.7 100.7 all-gather.7
  216.6 82.7 all-gather.9
  301.3 83.2 all-gather.11
where the time goes:
time: 642 us; the launch traced here: 641 us
  waiting for transfers between devices  292 us (45%)
  blocking collectives  154 us (24%)
  local copies, waits for them, and re-layouts  85.7 us (13%)
  other arithmetic  56.5 us (9%)
  starting transfers between devices  28.5 us (4%)
  between operations  14.1 us (2%)
  matrix products  10.2 us (2%)
    all_gather x1, waiting for transfers between devices, local(): selected = lax.all_gather(own_slots, 'ed', axis=1, tiled=True)  96.3 us
    all_gather x1, waiting for transfers between devices, local(): lax.all_gather(w_down[0], 'fsdp', axis=1, tiled=True)  85.3 us
    unnamed x1, blocking collectives  81.8 us
    all_to_all x1, blocking collectives, local(): lax.all_to_all(selected, 'fsdp', split_axis=1, concat_axis=2, tiled=True)  71.7 us
    all_gather x1, waiting for transfers between devices, local(): lax.all_gather(w_up, 'fsdp', axis=1, tiled=True)  66.1 us
    unnamed x2, other arithmetic  50.5 us
    all_to_all x1, waiting for transfers between devices, local(): lax.all_to_all(stacked, 'fsdp', split_axis=2, concat_axis=1, tiled=True)  42.9 us
    unnamed x19, local copies, waits for them, and re-layouts  34.1 us
  transfers between devices with their start and end apart: 10, of which 4 were waited for; matrix products, arithmetic and copies ran while one was open for 8% of the time, Pallas kernels for 0%

commit v1 on v0

--- a/solution.py
+++ b/solution.py
@@ -74,7 +74,10 @@
     whole_rows = columns_out(lax.all_gather(w_down[0], "fsdp", axis=1, tiled=True), jnp.int32(0))
     outputs_list = [whole_rows.astype(jnp.bfloat16)]
     stacked = jnp.stack(outputs_list)
-    exchanged = lax.all_to_all(stacked, "fsdp", split_axis=2, concat_axis=1, tiled=True)
+    exchanged = jnp.concatenate(
+        lax.all_to_all(jnp.stack(jnp.split(stacked, lax.axis_size("fsdp"), axis=2)), "fsdp", 0, 0),
+        axis=1,
+    )
     partial_out = exchanged.astype(jnp.float32)
     slot_out = lax.psum_scatter(
         partial_out.astype(jnp.bfloat16), "ed", scatter_dimension=1, tiled=True

time: 642 us -> 586 us (0.913)
  other arithmetic: 56.5 us -> 21.9 us
  local copies, waits for them, and re-layouts: 85.7 us -> 63.2 us
    unnamed x2 -> x1, other arithmetic: 50.5 us -> 15.8 us
    all_to_all x4 -> x0, local copies, waits for them, and re-layouts: 16 us -> none  [local(): lax.all_to_all(stacked, 'fsdp', split_axis=2, concat_axis=1, tiled=True)]
    another operation x5, local copies, waits for them, and re-layouts: 13.8 us -> 1.68 us  [the longest x1 1.57 us: local(): jnp.stack(jnp.split(stacked, lax.axis_size('fsdp'), axis=2))]
    unnamed x19 -> x29, local copies, waits for them, and re-layouts: 34.1 us -> 38.1 us
  transfers between devices with their start and end apart: 10 -> 10, of which waited for: 4 -> 4; matrix products, arithmetic and copies ran while one was open for 8% -> 9% of each run, Pallas kernels for 0% -> 0%
where the time goes in v1:
time: 586 us; the launch traced here: 585 us
  waiting for transfers between devices  294 us (50%)
  blocking collectives  154 us (26%)
  local copies, waits for them, and re-layouts  63.2 us (11%)
  starting transfers between devices  28.3 us (5%)
  other arithmetic  21.9 us (4%)
  between operations  14 us (2%)
  matrix products  10.3 us (2%)
    all_gather x1, waiting for transfers between devices, local(): selected = lax.all_gather(own_slots, 'ed', axis=1, tiled=True)  96.3 us
    all_gather x1, waiting for transfers between devices, local(): lax.all_gather(w_down[0], 'fsdp', axis=1, tiled=True)  85.3 us
    unnamed x1, blocking collectives  82 us
    all_to_all x1, blocking collectives, local(): lax.all_to_all(selected, 'fsdp', split_axis=1, concat_axis=2, tiled=True)  71.7 us
    all_gather x1, waiting for transfers between devices, local(): lax.all_gather(w_up, 'fsdp', axis=1, tiled=True)  66.1 us
    all_to_all x1, waiting for transfers between devices, local(): lax.all_to_all(jnp.stack(jnp.split(stacked, lax.axis_size('fsdp'), axis=2...  44.4 us
    unnamed x29, local copies, waits for them, and re-layouts  38.1 us
    unnamed x5, starting transfers between devices  24 us
  transfers between devices with their start and end apart: 10, of which 4 were waited for; matrix products, arithmetic and copies ran while one was open for 9% of the time, Pallas kernels for 0%

profile of v1, /device:TPU:1, one launch (start us, length us, event | category | flops | bytes accessed | tf_op | source)
XLA Modules:
  0.0 585.3 jit_solution(956691187740175053)
XLA Ops:
  8.1 3.0 convert_reduce_fusion
  15.4 96.3 %all-gather.6.cloned.1.call-done = bf16[1,2592,384]{2,0,1:T(2,128)(2,1)} async-done(((bf16[1,81,384]{2,0,1:T(2,128)(2,1)}), bf16[1,2592,384]{2,0,1:T(2,128)(2,1)}) %all-gather.6.cloned.1.call-update) | async-done | bytes 1990672 | tf_op jit(solution)/shard_map/all_gather | solution.py:54
  112.2 15.8 %reduce.14 = bf16[2592,384]{1,0:T(8,128)(2,1)S(1)} reduce(bf16[2592,1,384]{2,1,0:T(2,128)(2,1)} %bitcast.130, bf16[]{:T(256)} %broadcast.283), dimensions={1}, to_apply=%bitcast.117.reduce_sub_computation | reduce | bytes 3981314
  129.6 71.7 %all_to_all.20 = bf16[16,2,31104]{2,1,0:T(2,128)(2,1)S(1)} all-to-all(bf16[16,2,31104]{2,1,0:T(2,128)(2,1)} %reshape.467), channel_id=1, replica_groups=mesh['fsdp'=16,'ed'=32] {'fsdp'}, dimensions={0} | all-to-all | bytes 3981312 | tf_op jit(solution)/shard_map/all_to_all | solution.py:55
  201.2 8.9 %reshape.468 = bf16[2592,1,384]{2,1,0:T(2,128)(2,1)} reshape(bf16[16,2,31104]{2,1,0:T(2,128)(2,1)S(1)} %all_to_all.20) | data formatting | bytes 3981312
  210.2 17.6 %bitcast_reduce_fusion = bf16[2592,384]{1,0:T(8,128)(2,1)} fusion(bf16[2592,1,384]{2,1,0:T(2,128)(2,1)} %reshape.468), kind=kLoop, calls=%fused_computation.77 | loop fusion | bytes 3981312 | tf_op jit(solution)/shard_map/all_to_all | solution.py:55
  227.8 1.8 all_to_all.15
  230.6 2.7 fusion.5
  233.3 66.1 %all-gather.10.cloned.1.call-done = bf16[1,6144,256]{2,1,0:T(8,128)(2,1)} async-done(((bf16[1,384,256]{2,1,0:T(8,128)(2,1)}), bf16[1,6144,256]{2,1,0:T(8,128)(2,1)}) %all-gather.10.cloned.1.call-update) | async-done | bytes 3145744 | tf_op jit(solution)/shard_map/all_gather | solution.py:65
  299.3 85.3 %all-gather.12.cloned.1.call-done = bf16[1,256,6144]{2,1,0:T(8,128)(2,1)} async-done(((bf16[1,256,384]{2,1,0:T(8,128)(2,1)}), bf16[1,256,6144]{2,1,0:T(8,128)(2,1)}) %all-gather.12.cloned.1.call-update) | async-done | bytes 3145744 | tf_op jit(solution)/shard_map/all_gather | solution.py:74
  384.6 6.6 %fusion.1 = bf16[1,162,6144]{2,1,0:T(8,128)(2,1)} fusion(bf16[1,256,6144]{2,1,0:T(8,128)(2,1)} %all-gather.12.cloned.1.call-done, bf16[162,6144]{1,0:T(8,128)(2,1)S(1)} %bitcast.126, bf16[1,6144,256]{2,1,0:T(8,128)(2,1)} %all-gather.10.cloned.1.call-done, f32[162,256]{1,0:T(8,128)S(1)} %fusion.5), kind=kOutput, calls=%fused_computation.2 | convolution fusion | flops 1020460032 | bytes 10438656 | tf_op jit(solution)/shard_map/dot_general | solution.py:72
  391.2 1.6 fusion.35
  399.0 1.6 fusion.30
  402.1 1.6 fusion.28
  403.7 1.6 fusion.27
  411.5 1.6 fusion.22
  414.7 1.6 fusion.20
  416.3 4.2 all-to-all-start.1
  420.5 44.4 %all-to-all-done.1 = bf16[16,1,162,384]{3,2,1,0:T(8,128)(2,1)S(1)} async-done(((bf16[16,1,162,384]{3,2,1,0:T(8,128)(2,1)}), bf16[16,1,162,384]{3,2,1,0:T(8,128)(2,1)S(1)}, u32[]{:S(2)}, u32[]{:S(2)}) %all-to-all-start.1) | async-done | bytes 1990688 | tf_op jit(solution)/shard_map/all_to_all | solution.py:78
  466.4 82.0 %fusion = bf16[96,384]{1,0:T(8,128)(2,1)S(1)} fusion(bf16[1,2592,384]{2,1,0:T(8,128)(2,1)} %reshape.448), kind=kCustom, calls=%all-reduce-scatter | all-reduce-scatter fusion | flops 1179649 | bytes 2066432
  548.5 3.4 collective-permute-start
  555.8 16.7 %collective-permute-start.4 = (bf16[81,384]{1,0:T(8,128)(2,1)S(1)}, bf16[81,384]{1,0:T(8,128)(2,1)S(1)}, u32[]{:S(2)}, u32[]{:S(2)}) collective-permute-start(bf16[81,384]{1,0:T(8,128)(2,1)S(1)} %slice.16), channel_id=1, source_target_pairs={{0,5},{1,6},{2,7},{3,8},{4,9},{5,10},{6,11},{7,12},{8,13},{9,14},{... | collective-permute-start | bytes 186632
  572.5 1.7 convert_multiply_fusion
  576.2 1.6 concatenate.3
  (61 shorter events, 32.3 us)
Async XLA Ops:
  6.5 4.6 copy-start
  6.5 105.1 %all-gather.6.cloned.1.call-start = ((), (), s32[]{:S(2)}) async-start(), calls=%async_computation.2 | async-start | bytes 4105728 | tf_op jit(solution)/shard_map/all_gather | solution.py:54
  13.3 217.3 %all-gather.8.cloned.1.call-start = ((), (), s32[]{:S(2)}) async-start(), calls=%async_computation.3 | async-start | bytes 3342336 | tf_op jit(solution)/shard_map/all_gather | solution.py:59
  14.1 285.3 %all-gather.10.cloned.1.call-start = ((), (), s32[]{:S(2)}) async-start(), calls=%async_computation.4 | async-start | bytes 3342336 | tf_op jit(solution)/shard_map/all_gather | solution.py:65
  14.8 369.8 %all-gather.12.cloned.1.call-start = ((), (), s32[]{:S(2)}) async-start(), calls=%async_computation.5 | async-start | bytes 3342336 | tf_op jit(solution)/shard_map/all_gather | solution.py:74
  416.3 4.2 copy-start.1
  416.3 4.2 copy-start.2
  416.3 48.6 %all-to-all-start.1 = ((bf16[16,1,162,384]{3,2,1,0:T(8,128)(2,1)}), bf16[16,1,162,384]{3,2,1,0:T(8,128)(2,1)S(1)}, u32[]{:S(2)}, u32[]{:S(2)}) async-start(bf16[16,1,162,384]{3,2,1,0:T(8,128)(2,1)} %fusion.20), calls=%async_computation.1 | async-start | bytes 4128768 | tf_op jit(solution)/shard_map/all_to_all | solution.py:78
  548.5 27.7 %collective-permute-start = (bf16[96,384]{1,0:T(8,128)(2,1)S(1)}, bf16[96,384]{1,0:T(8,128)(2,1)S(1)}, u32[]{:S(2)}, u32[]{:S(2)}) collective-permute-start(bf16[96,384]{1,0:T(8,128)(2,1)S(1)} %fusion), channel_id=1, source_target_pairs={{0,1},{1,2},{2,3},{3,4},{4,5},{5,6},{6,7},{7,8},{8,9},{9,10},{10,1... | collective-permute-start | bytes 221192
  551.9 24.2 %collective-permute-start.1 = (bf16[96,384]{1,0:T(8,128)(2,1)S(1)}, bf16[96,384]{1,0:T(8,128)(2,1)S(1)}, u32[]{:S(2)}, u32[]{:S(2)}) collective-permute-start(bf16[96,384]{1,0:T(8,128)(2,1)S(1)} %fusion), channel_id=1, source_target_pairs={{0,2},{1,3},{2,4},{3,5},{4,6},{5,7},{6,8},{7,9},{8,10},{9,11},{10,... | collective-permute-start | bytes 221192
  553.2 22.9 %collective-permute-start.2 = (bf16[96,384]{1,0:T(8,128)(2,1)S(1)}, bf16[96,384]{1,0:T(8,128)(2,1)S(1)}, u32[]{:S(2)}, u32[]{:S(2)}) collective-permute-start(bf16[96,384]{1,0:T(8,128)(2,1)S(1)} %fusion), channel_id=1, source_target_pairs={{0,3},{1,4},{2,5},{3,6},{4,7},{5,8},{6,9},{7,10},{8,11},{9,12},{10... | collective-permute-start | bytes 221192
  554.5 21.6 %collective-permute-start.3 = (bf16[96,384]{1,0:T(8,128)(2,1)S(1)}, bf16[96,384]{1,0:T(8,128)(2,1)S(1)}, u32[]{:S(2)}, u32[]{:S(2)}) collective-permute-start(bf16[96,384]{1,0:T(8,128)(2,1)S(1)} %fusion), channel_id=1, source_target_pairs={{0,4},{1,5},{2,6},{3,7},{4,8},{5,9},{6,10},{7,11},{8,12},{9,13},{1... | collective-permute-start | bytes 221192
  555.8 20.3 %collective-permute-start.4 = (bf16[81,384]{1,0:T(8,128)(2,1)S(1)}, bf16[81,384]{1,0:T(8,128)(2,1)S(1)}, u32[]{:S(2)}, u32[]{:S(2)}) collective-permute-start(bf16[81,384]{1,0:T(8,128)(2,1)S(1)} %slice.16), channel_id=1, source_target_pairs={{0,5},{1,6},{2,7},{3,8},{4,9},{5,10},{6,11},{7,12},{8,13},{9,14},{... | collective-permute-start | bytes 186632
Sparse Core Ops, SparseCore 0:
  13.4 98.1 all-gather.5
  113.7 100.7 all-gather.7
  216.6 82.7 all-gather.9
  301.3 83.2 all-gather.11
